TPU v7x, 512 devices: a whole 4x8x8 slice. The times are simulated.
512 devices in a mesh: wide: 64 (over y, z), narrow: 8 (over x, core).
Axes of the slice: x: 4, y: 8, z: 8, core: 2. Of those that a mesh axis runs over, the one named last changes fastest.
Arguments:
- right_side: bfloat16 [4, 1024, 512], P(None, 'wide'), may hold values from -6 to 6
- partial_in: float32 [8, 4, 1024, 512], P('narrow', None, 'wide'), may hold values from -6 to 6
- window_factor: bfloat16 [4, 1024, 4, 1024], P(None, 'wide', None, 'narrow'), may hold values from -0.09375 to 0.09375
- inverse_t: bfloat16 [4, 1024, 1024], P(None, 'wide', 'narrow'), as said below
- trailing_factor: bfloat16 [131072, 4, 1024], P('wide', None, 'narrow'), may hold values from -0.09375 to 0.09375
Outputs:
- solved: bfloat16 [4, 1024, 512], P(None, 'narrow')
- trailing: float32 [131072, 512], P(('wide', 'narrow'))
Inputs may be any that keep to these rules, and one draw needn't show every extreme that they name: inverse_t[k] is the transpose of the inverse of the k-th diagonal block of the lower-triangular factor: entry [k, j, i] is zero where j > i.
All inputs are finite; a program needn't handle non-finite values.
Results may differ from a plain program's by a relative error of at most 0.012.
Values may be sent and summed in bfloat16 or wider, within the bound.
No kernel may reach another device: no remote copies, remote signals or barrier semaphores. Data moves between devices by JAX's collectives and lax.ppermute only.
A program may use at most 64 MiB of HBM per device.

v0:
```python
import jax
import jax.numpy as jnp
from jax import lax
from jax.sharding import PartitionSpec as P


def per_device(right_side, partial_in, window_factor, inverse_t, trailing_factor):
    steps_count = right_side.shape[0]
    col_width = inverse_t.shape[2]
    rhs_width = right_side.shape[2]
    trail_rows = trailing_factor.shape[0]
    solved_list = []
    for block in range(steps_count):
        fanned = partial_in[0, block]
        for prior in range(block):
            fanned = fanned + jnp.dot(
                window_factor[block, :, prior, :],
                solved_list[prior],
                preferred_element_type=jnp.float32,
            )
        fanned = lax.psum(fanned, "narrow")
        residue = (right_side[block].astype(jnp.float32) - fanned).astype(jnp.bfloat16)
        solution = lax.dot_general(
            lax.all_gather(inverse_t[block], "wide", axis=0, tiled=True),
            lax.all_gather(residue, "wide", axis=0, tiled=True),
            (((0,), (0,)), ((), ())),
            preferred_element_type=jnp.float32,
        )
        solution = solution.astype(jnp.bfloat16)
        solved_list.append(solution)
    solved = jnp.stack(solved_list)
    flat_factor = trailing_factor.reshape(trail_rows, steps_count * col_width)
    flat_solved = solved.reshape(steps_count * col_width, rhs_width)
    trailing = lax.psum_scatter(
        jnp.dot(flat_factor, flat_solved, preferred_element_type=jnp.float32),
        "narrow",
        scatter_dimension=0,
        tiled=True,
    )
    return (solved, trailing)


def solution(mesh):
    placed = (
        P(None, "wide", None),
        P("narrow", None, "wide", None),
        P(None, "wide", None, "narrow"),
        P(None, "wide", "narrow"),
        P("wide", None, "narrow"),
    )
    return jax.shard_map(
        per_device,
        mesh=mesh,
        in_specs=placed,
        out_specs=(P(None, "narrow", None), P(("wide", "narrow"), None)),
        check_vma=False,
    )
```

profile of v0, /device:TPU:8, one launch (start us, length us, event | category | flops | bytes accessed | tf_op | source)
XLA Modules:
  0.0 483.0 jit_solution(5871402175136502424)
XLA Ops:
  7.2 0.9 slice_bitcast_fusion
  8.2 25.6 %psum.28 = f32[16,512]{1,0:T(8,128)S(1)} all-reduce(f32[16,512]{1,0:T(8,128)S(1)} %slice_bitcast_fusion), channel_id=1, replica_groups=mesh['wide'=64,'narrow'=8] {'narrow'}, use_global_device_ids=true, to_apply=%region_0.0 | all-reduce | flops 8192 | bytes 65536 | tf_op jit(solution)/shard_map/psum | solution.py:21
  33.8 1.3 fusion.15
  35.2 0.7 fusion.17
  35.9 56.0 %all-gather = bf16[1,1024,128]{2,1,0:T(8,128)(2,1)S(1)} all-gather(bf16[1,16,128]{2,1,0:T(8,128)(2,1)S(1)} %get-tuple-element.14), channel_id=2, replica_groups=mesh['wide'=64,'narrow'=8] {'wide'}, dimensions={1}, use_global_device_ids=true | all-gather | bytes 266240 | tf_op jit(solution)/shard_map/all_gather | solution.py:24
  91.9 0.9 fusion.16
  92.8 26.1 %all-gather.9.cloned.1.call-done = bf16[1024,512]{1,0:T(8,128)(2,1)} async-done(((bf16[16,512]{1,0:T(8,128)(2,1)}), bf16[1024,512]{1,0:T(8,128)(2,1)}) %all-gather.9.cloned.1.call-update) | async-done | bytes 1048592 | tf_op jit(solution)/shard_map/all_gather | solution.py:25
  118.9 1.7 convolution_convert_fusion.3
  120.6 0.9 fusion.7
  121.5 23.6 %psum.29 = f32[16,512]{1,0:T(8,128)S(1)} all-reduce(f32[16,512]{1,0:T(8,128)S(1)} %fusion.7), channel_id=1, replica_groups=mesh['wide'=64,'narrow'=8] {'narrow'}, use_global_device_ids=true, to_apply=%region_1.0 | all-reduce | flops 8192 | bytes 65536 | tf_op jit(solution)/shard_map/psum | solution.py:21
  145.1 0.6 fusion.14
  145.8 48.2 %all-gather.1 = bf16[1,1024,128]{2,1,0:T(8,128)(2,1)S(1)} all-gather(bf16[1,16,128]{2,1,0:T(8,128)(2,1)S(1)} %get-tuple-element.13), channel_id=3, replica_groups=mesh['wide'=64,'narrow'=8] {'wide'}, dimensions={1}, use_global_device_ids=true | all-gather | bytes 266240 | tf_op jit(solution)/shard_map/all_gather | solution.py:24
  194.2 28.4 %all-gather.11.cloned.1.call-done = bf16[1024,512]{1,0:T(8,128)(2,1)} async-done(((bf16[16,512]{1,0:T(8,128)(2,1)}), bf16[1024,512]{1,0:T(8,128)(2,1)}) %all-gather.11.cloned.1.call-update) | async-done | bytes 1048592 | tf_op jit(solution)/shard_map/all_gather | solution.py:25
  222.6 1.7 convolution_convert_fusion.2
  224.3 0.1 fusion.5
  224.4 23.6 %psum.30 = f32[16,512]{1,0:T(8,128)S(1)} all-reduce(f32[16,512]{1,0:T(8,128)S(1)} %fusion.5), channel_id=1, replica_groups=mesh['wide'=64,'narrow'=8] {'narrow'}, use_global_device_ids=true, to_apply=%region_2.0 | all-reduce | flops 8192 | bytes 65536 | tf_op jit(solution)/shard_map/psum | solution.py:21
  248.0 0.6 fusion.13
  248.7 48.2 %all-gather.2 = bf16[1,1024,128]{2,1,0:T(8,128)(2,1)S(1)} all-gather(bf16[1,16,128]{2,1,0:T(8,128)(2,1)S(1)} %get-tuple-element.15), channel_id=4, replica_groups=mesh['wide'=64,'narrow'=8] {'wide'}, dimensions={1}, use_global_device_ids=true | all-gather | bytes 266240 | tf_op jit(solution)/shard_map/all_gather | solution.py:24
  296.9 0.2 fusion.4
  297.1 0.1 fusion.3
  297.2 28.3 %all-gather.13.cloned.1.call-done = bf16[1024,512]{1,0:T(8,128)(2,1)} async-done(((bf16[16,512]{1,0:T(8,128)(2,1)}), bf16[1024,512]{1,0:T(8,128)(2,1)}) %all-gather.13.cloned.1.call-update) | async-done | bytes 1048592 | tf_op jit(solution)/shard_map/all_gather | solution.py:25
  325.5 1.7 convolution_convert_fusion.1
  327.2 0.1 fusion.2
  327.4 23.6 %psum.31 = f32[16,512]{1,0:T(8,128)S(1)} all-reduce(f32[16,512]{1,0:T(8,128)S(1)} %fusion.2), channel_id=1, replica_groups=mesh['wide'=64,'narrow'=8] {'narrow'}, use_global_device_ids=true, to_apply=%region_3.0 | all-reduce | flops 8192 | bytes 65536 | tf_op jit(solution)/shard_map/psum | solution.py:21
  351.0 0.6 fusion.12
  351.7 48.2 %all-gather.3 = bf16[1,1024,128]{2,1,0:T(8,128)(2,1)S(1)} all-gather(bf16[1,16,128]{2,1,0:T(8,128)(2,1)S(1)} %get-tuple-element.12), channel_id=5, replica_groups=mesh['wide'=64,'narrow'=8] {'wide'}, dimensions={1}, use_global_device_ids=true | all-gather | bytes 266240 | tf_op jit(solution)/shard_map/all_gather | solution.py:24
  399.9 28.6 %all-gather.15.cloned.1.call-done = bf16[1024,512]{1,0:T(8,128)(2,1)} async-done(((bf16[16,512]{1,0:T(8,128)(2,1)}), bf16[1024,512]{1,0:T(8,128)(2,1)}) %all-gather.15.cloned.1.call-update) | async-done | bytes 1048592 | tf_op jit(solution)/shard_map/all_gather | solution.py:25
  428.5 1.7 fusion.1
  430.2 3.2 convolution_bitcast_fusion
  433.5 1.0 copy.17
  434.5 39.9 %reduce-scatter.2.cloned.1.call-done = f32[256,512]{0,1:T(8,128)} async-done(((f32[2048,512]{0,1:T(8,128)}), f32[256,512]{0,1:T(8,128)}) %reduce-scatter.2.cloned.1.call-update) | async-done | bytes 524304 | tf_op jit(solution)/shard_map/reduce_scatter | solution.py:34
  474.5 2.0 copy.18
  (18 shorter events, 0.5 us)
Async XLA Ops:
  7.2 423.0 %copy-start = (bf16[2048,4,128]{2,1,0:T(4,128)(2,1)S(1)}, bf16[2048,4,128]{2,1,0:T(4,128)(2,1)}, u32[]{:S(2)}) copy-start(bf16[2048,4,128]{2,1,0:T(4,128)(2,1)} %param.9) | copy-start | bytes 6291460
  7.2 186.8 %copy-start.1 = (f32[1,4,16,512]{3,2,1,0:T(8,128)S(1)}, f32[1,4,16,512]{3,2,1,0:T(8,128)}, u32[]{:S(2)}) copy-start(f32[1,4,16,512]{3,2,1,0:T(8,128)} %param.6) | copy-start | bytes 393220
  7.2 137.9 %copy-start.2 = (bf16[4,16,512]{2,1,0:T(8,128)(2,1)S(1)}, bf16[4,16,512]{2,1,0:T(8,128)(2,1)}, u32[]{:S(2)}) copy-start(bf16[4,16,512]{2,1,0:T(8,128)(2,1)} %param.5) | copy-start | bytes 196612
  7.2 111.7 %all-gather.9.cloned.1.call-start = ((), (), s32[]{:S(2)}) async-start(), calls=%async_computation.1 | async-start | bytes 1064960 | tf_op jit(solution)/shard_map/all_gather | solution.py:25
  35.1 187.4 %all-gather.11.cloned.1.call-start = ((), (), s32[]{:S(2)}) async-start(), calls=%async_computation.2 | async-start | bytes 1064960 | tf_op jit(solution)/shard_map/all_gather | solution.py:25
  145.7 179.8 %all-gather.13.cloned.1.call-start = ((), (), s32[]{:S(2)}) async-start(), calls=%async_computation.3 | async-start | bytes 1064960 | tf_op jit(solution)/shard_map/all_gather | solution.py:25
  248.7 179.8 %all-gather.15.cloned.1.call-start = ((), (), s32[]{:S(2)}) async-start(), calls=%async_computation.4 | async-start | bytes 1064960 | tf_op jit(solution)/shard_map/all_gather | solution.py:25
  351.6 122.8 %reduce-scatter.2.cloned.1.call-start = ((), (), s32[]{:S(2)}) async-start(), calls=%async_computation.5 | async-start | bytes 4718592 | tf_op jit(solution)/shard_map/reduce_scatter | solution.py:34
Sparse Core Ops, SparseCore 0:
  35.2 83.6 all-gather.8
  145.9 76.6 all-gather.10
  248.8 76.6 all-gather.12
  351.7 76.6 all-gather.14
  433.6 40.8 reduce-scatter.1
where the time goes:
time: 484 us; the launch traced here: 483 us
  blocking collectives  297 us (61%)
  waiting for transfers between devices  151 us (31%)
  between operations  13.9 us (3%)
  matrix products  11.7 us (2%)
  local copies, waits for them, and re-layouts  5.6 us (1%)
    all_gather x4, blocking collectives, per_device(): lax.all_gather(inverse_t[block], 'wide', axis=0, tiled=True)  201 us
    all_gather x4, waiting for transfers between devices, per_device(): lax.all_gather(residue, 'wide', axis=0, tiled=True)  111 us
    psum x4, blocking collectives, per_device(): fanned = lax.psum(fanned, 'narrow')  96.4 us
    reduce_scatter x1, waiting for transfers between devices, per_device(): lax.psum_scatter(jnp.dot(flat_factor, flat_solved, preferred_element_type...  39.9 us
  transfers between devices with their start and end apart: 5, of which 5 were waited for; matrix products, arithmetic and copies ran while one was open for 1% of the time, Pallas kernels for 0%

commit v1 on v0

--- a/solution.py
+++ b/solution.py
@@ -18,7 +18,9 @@
                 solved_list[prior],
                 preferred_element_type=jnp.float32,
             )
-        fanned = lax.psum(fanned, "narrow")
+        fanned = fanned
+        for hop in (1, 2, 4):
+            fanned = fanned + lax.ppermute(fanned, "narrow", [(dev, dev ^ hop) for dev in range(8)])
         residue = (right_side[block].astype(jnp.float32) - fanned).astype(jnp.bfloat16)
         solution = lax.dot_general(
             lax.all_gather(inverse_t[block], "wide", axis=0, tiled=True),

time: 484 us -> 462 us (0.955)
  blocking collectives: 297 us -> 201 us
  starting transfers between devices: 0.21 us -> 40.9 us
  waiting for transfers between devices: 151 us -> 185 us
    psum x4 -> x0, blocking collectives: 96.4 us -> none  [per_device(): fanned = lax.psum(fanned, 'narrow')]
    ppermute x0 -> x12, starting transfers between devices: none -> 40.7 us  [per_device(): lax.ppermute(fanned, 'narrow', [(dev, dev ^ hop) for dev in range(8)])]
    ppermute x0 -> x12, waiting for transfers between devices: none -> 24 us  [per_device(): lax.ppermute(fanned, 'narrow', [(dev, dev ^ hop) for dev in range(8)])]
    all_gather x4, waiting for transfers between devices: 111 us -> 121 us  [per_device(): lax.all_gather(residue, 'wide', axis=0, tiled=True)]
  transfers between devices with their start and end apart: 5 -> 17, of which waited for: 5 -> 17; matrix products, arithmetic and copies ran while one was open for 1% -> 1% of each run, Pallas kernels for 0% -> 0%
where the time goes in v1:
time: 462 us; the launch traced here: 461 us
  blocking collectives  201 us (44%)
  waiting for transfers between devices  185 us (40%)
  starting transfers between devices  40.9 us (9%)
  between operations  14 us (3%)
  matrix products  10.9 us (2%)
  local copies, waits for them, and re-layouts  5.6 us (1%)
    all_gather x4, blocking collectives, per_device(): lax.all_gather(inverse_t[block], 'wide', axis=0, tiled=True)  201 us
    all_gather x4, waiting for transfers between devices, per_device(): lax.all_gather(residue, 'wide', axis=0, tiled=True)  121 us
    ppermute x12, starting transfers between devices, per_device(): lax.ppermute(fanned, 'narrow', [(dev, dev ^ hop) for dev in range(8)])  40.7 us
    reduce_scatter x1, waiting for transfers between devices, per_device(): lax.psum_scatter(jnp.dot(flat_factor, flat_solved, preferred_element_type...  39.9 us
    ppermute x12, waiting for transfers between devices, per_device(): lax.ppermute(fanned, 'narrow', [(dev, dev ^ hop) for dev in range(8)])  24 us
  transfers between devices with their start and end apart: 17, of which 17 were waited for; matrix products, arithmetic and copies ran while one was open for 1% of the time, Pallas kernels for 0%

profile of v1, /device:TPU:8, one launch (start us, length us, event | category | flops | bytes accessed | tf_op | source)
XLA Modules:
  0.0 461.1 jit_solution(15372348267076694876)
XLA Ops:
  8.2 1.9 collective-permute-start
  12.0 3.4 collective-permute-start.1
  15.4 2.4 collective-permute-done.1
  17.8 4.9 %collective-permute-start.2 = (f32[16,512]{1,0:T(8,128)S(1)}, f32[16,512]{1,0:T(8,128)S(1)}, u32[]{:S(2)}, u32[]{:S(2)}) collective-permute-start(f32[16,512]{1,0:T(8,128)S(1)} %add.57), channel_id=1, source_target_pairs={{0,4},{1,5},{2,6},{3,7},{4,0},{5,1},{6,2},{7,3},{8,12},{9,13},{10,... | collective-permute-start | bytes 98312 | tf_op jit(solution)/shard_map/ppermute | solution.py:23
  22.7 2.4 collective-permute-done.2
  27.3 56.0 %all-gather = bf16[1,1024,128]{2,1,0:T(8,128)(2,1)S(1)} all-gather(bf16[1,16,128]{2,1,0:T(8,128)(2,1)S(1)} %get-tuple-element.14), channel_id=2, replica_groups=mesh['wide'=64,'narrow'=8] {'wide'}, dimensions={1}, use_global_device_ids=true | all-gather | bytes 266240 | tf_op jit(solution)/shard_map/all_gather | solution.py:26
  84.1 28.6 %all-gather.9.cloned.1.call-done = bf16[1024,512]{1,0:T(8,128)(2,1)} async-done(((bf16[16,512]{1,0:T(8,128)(2,1)}), bf16[1024,512]{1,0:T(8,128)(2,1)}) %all-gather.9.cloned.1.call-update) | async-done | bytes 1048592 | tf_op jit(solution)/shard_map/all_gather | solution.py:27
  114.6 1.9 collective-permute-start.3
  117.7 3.4 collective-permute-start.4
  121.1 2.4 collective-permute-done.4
  123.5 4.9 %collective-permute-start.5 = (f32[16,512]{1,0:T(8,128)S(1)}, f32[16,512]{1,0:T(8,128)S(1)}, u32[]{:S(2)}, u32[]{:S(2)}) collective-permute-start(f32[16,512]{1,0:T(8,128)S(1)} %add.61), channel_id=1, source_target_pairs={{0,4},{1,5},{2,6},{3,7},{4,0},{5,1},{6,2},{7,3},{8,12},{9,13},{10,... | collective-permute-start | bytes 98312 | tf_op jit(solution)/shard_map/ppermute | solution.py:23
  128.4 2.4 collective-permute-done.5
  131.5 48.2 %all-gather.1 = bf16[1,1024,128]{2,1,0:T(8,128)(2,1)S(1)} all-gather(bf16[1,16,128]{2,1,0:T(8,128)(2,1)S(1)} %get-tuple-element.13), channel_id=3, replica_groups=mesh['wide'=64,'narrow'=8] {'wide'}, dimensions={1}, use_global_device_ids=true | all-gather | bytes 266240 | tf_op jit(solution)/shard_map/all_gather | solution.py:26
  179.8 30.8 %all-gather.11.cloned.1.call-done = bf16[1024,512]{1,0:T(8,128)(2,1)} async-done(((bf16[16,512]{1,0:T(8,128)(2,1)}), bf16[1024,512]{1,0:T(8,128)(2,1)}) %all-gather.11.cloned.1.call-update) | async-done | bytes 1048592 | tf_op jit(solution)/shard_map/all_gather | solution.py:27
  212.5 1.9 collective-permute-start.6
  215.6 3.4 collective-permute-start.7
  219.0 2.4 collective-permute-done.7
  221.4 4.9 %collective-permute-start.8 = (f32[16,512]{1,0:T(8,128)S(1)}, f32[16,512]{1,0:T(8,128)S(1)}, u32[]{:S(2)}, u32[]{:S(2)}) collective-permute-start(f32[16,512]{1,0:T(8,128)S(1)} %add.66), channel_id=1, source_target_pairs={{0,4},{1,5},{2,6},{3,7},{4,0},{5,1},{6,2},{7,3},{8,12},{9,13},{10,... | collective-permute-start | bytes 98312 | tf_op jit(solution)/shard_map/ppermute | solution.py:23
  226.3 2.4 collective-permute-done.8
  229.4 48.2 %all-gather.2 = bf16[1,1024,128]{2,1,0:T(8,128)(2,1)S(1)} all-gather(bf16[1,16,128]{2,1,0:T(8,128)(2,1)S(1)} %get-tuple-element.15), channel_id=4, replica_groups=mesh['wide'=64,'narrow'=8] {'wide'}, dimensions={1}, use_global_device_ids=true | all-gather | bytes 266240 | tf_op jit(solution)/shard_map/all_gather | solution.py:26
  277.9 30.7 %all-gather.13.cloned.1.call-done = bf16[1024,512]{1,0:T(8,128)(2,1)} async-done(((bf16[16,512]{1,0:T(8,128)(2,1)}), bf16[1024,512]{1,0:T(8,128)(2,1)}) %all-gather.13.cloned.1.call-update) | async-done | bytes 1048592 | tf_op jit(solution)/shard_map/all_gather | solution.py:27
  308.6 1.7 convolution_convert_fusion.1
  310.5 1.9 collective-permute-start.9
  313.6 3.4 collective-permute-start.10
  316.9 2.4 collective-permute-done.10
  319.4 4.9 %collective-permute-start.11 = (f32[16,512]{1,0:T(8,128)S(1)}, f32[16,512]{1,0:T(8,128)S(1)}, u32[]{:S(2)}, u32[]{:S(2)}) collective-permute-start(f32[16,512]{1,0:T(8,128)S(1)} %add.72), channel_id=1, source_target_pairs={{0,4},{1,5},{2,6},{3,7},{4,0},{5,1},{6,2},{7,3},{8,12},{9,13},{10,... | collective-permute-start | bytes 98312 | tf_op jit(solution)/shard_map/ppermute | solution.py:23
  324.3 2.4 collective-permute-done.11
  327.4 48.2 %all-gather.3 = bf16[1,1024,128]{2,1,0:T(8,128)(2,1)S(1)} all-gather(bf16[1,16,128]{2,1,0:T(8,128)(2,1)S(1)} %get-tuple-element.12), channel_id=5, replica_groups=mesh['wide'=64,'narrow'=8] {'wide'}, dimensions={1}, use_global_device_ids=true | all-gather | bytes 266240 | tf_op jit(solution)/shard_map/all_gather | solution.py:26
  375.6 31.0 %all-gather.15.cloned.1.call-done = bf16[1024,512]{1,0:T(8,128)(2,1)} async-done(((bf16[16,512]{1,0:T(8,128)(2,1)}), bf16[1024,512]{1,0:T(8,128)(2,1)}) %all-gather.15.cloned.1.call-update) | async-done | bytes 1048592 | tf_op jit(solution)/shard_map/all_gather | solution.py:27
  408.3 3.3 convolution_bitcast_fusion
  412.6 39.9 %reduce-scatter.2.cloned.1.call-done = f32[256,512]{0,1:T(8,128)} async-done(((f32[2048,512]{0,1:T(8,128)}), f32[256,512]{0,1:T(8,128)}) %reduce-scatter.2.cloned.1.call-update) | async-done | bytes 524304 | tf_op jit(solution)/shard_map/reduce_scatter | solution.py:36
  452.6 2.0 copy.18
  (46 shorter events, 18.5 us)
Async XLA Ops:
  7.2 401.1 %copy-start = (bf16[2048,4,128]{2,1,0:T(4,128)(2,1)S(1)}, bf16[2048,4,128]{2,1,0:T(4,128)(2,1)}, u32[]{:S(2)}) copy-start(bf16[2048,4,128]{2,1,0:T(4,128)(2,1)} %param.9) | copy-start | bytes 6291460
  7.2 107.2 %copy-start.1 = (f32[1,4,16,512]{3,2,1,0:T(8,128)S(1)}, f32[1,4,16,512]{3,2,1,0:T(8,128)}, u32[]{:S(2)}) copy-start(f32[1,4,16,512]{3,2,1,0:T(8,128)} %param.6) | copy-start | bytes 393220
  7.2 123.6 %copy-start.2 = (bf16[4,16,512]{2,1,0:T(8,128)(2,1)S(1)}, bf16[4,16,512]{2,1,0:T(8,128)(2,1)}, u32[]{:S(2)}) copy-start(bf16[4,16,512]{2,1,0:T(8,128)(2,1)} %param.5) | copy-start | bytes 196612
  7.2 105.5 %all-gather.9.cloned.1.call-start = ((), (), s32[]{:S(2)}) async-start(), calls=%async_computation.1 | async-start | bytes 1064960 | tf_op jit(solution)/shard_map/all_gather | solution.py:27
  8.2 3.1 collective-permute-start
  12.0 5.8 %collective-permute-start.1 = (f32[16,512]{1,0:T(8,128)S(1)}, f32[16,512]{1,0:T(8,128)S(1)}, u32[]{:S(2)}, u32[]{:S(2)}) collective-permute-start(f32[16,512]{1,0:T(8,128)S(1)} %fusion.16), channel_id=1, source_target_pairs={{0,2},{1,3},{2,0},{3,1},{4,6},{5,7},{6,4},{7,5},{8,10},{9,11},{10,... | collective-permute-start | bytes 98312 | tf_op jit(solution)/shard_map/ppermute | solution.py:23
  17.8 7.3 %collective-permute-start.2 = (f32[16,512]{1,0:T(8,128)S(1)}, f32[16,512]{1,0:T(8,128)S(1)}, u32[]{:S(2)}, u32[]{:S(2)}) collective-permute-start(f32[16,512]{1,0:T(8,128)S(1)} %add.57), channel_id=1, source_target_pairs={{0,4},{1,5},{2,6},{3,7},{4,0},{5,1},{6,2},{7,3},{8,12},{9,13},{10,... | collective-permute-start | bytes 98312 | tf_op jit(solution)/shard_map/ppermute | solution.py:23
  26.5 184.2 %all-gather.11.cloned.1.call-start = ((), (), s32[]{:S(2)}) async-start(), calls=%async_computation.2 | async-start | bytes 1064960 | tf_op jit(solution)/shard_map/all_gather | solution.py:27
  114.6 3.1 collective-permute-start.3
  117.7 5.8 %collective-permute-start.4 = (f32[16,512]{1,0:T(8,128)S(1)}, f32[16,512]{1,0:T(8,128)S(1)}, u32[]{:S(2)}, u32[]{:S(2)}) collective-permute-start(f32[16,512]{1,0:T(8,128)S(1)} %add.60), channel_id=1, source_target_pairs={{0,2},{1,3},{2,0},{3,1},{4,6},{5,7},{6,4},{7,5},{8,10},{9,11},{10,... | collective-permute-start | bytes 98312 | tf_op jit(solution)/shard_map/ppermute | solution.py:23
  123.5 7.3 %collective-permute-start.5 = (f32[16,512]{1,0:T(8,128)S(1)}, f32[16,512]{1,0:T(8,128)S(1)}, u32[]{:S(2)}, u32[]{:S(2)}) collective-permute-start(f32[16,512]{1,0:T(8,128)S(1)} %add.61), channel_id=1, source_target_pairs={{0,4},{1,5},{2,6},{3,7},{4,0},{5,1},{6,2},{7,3},{8,12},{9,13},{10,... | collective-permute-start | bytes 98312 | tf_op jit(solution)/shard_map/ppermute | solution.py:23
  131.4 177.2 %all-gather.13.cloned.1.call-start = ((), (), s32[]{:S(2)}) async-start(), calls=%async_computation.3 | async-start | bytes 1064960 | tf_op jit(solution)/shard_map/all_gather | solution.py:27
  212.5 3.1 collective-permute-start.6
  215.6 5.8 %collective-permute-start.7 = (f32[16,512]{1,0:T(8,128)S(1)}, f32[16,512]{1,0:T(8,128)S(1)}, u32[]{:S(2)}, u32[]{:S(2)}) collective-permute-start(f32[16,512]{1,0:T(8,128)S(1)} %add.65), channel_id=1, source_target_pairs={{0,2},{1,3},{2,0},{3,1},{4,6},{5,7},{6,4},{7,5},{8,10},{9,11},{10,... | collective-permute-start | bytes 98312 | tf_op jit(solution)/shard_map/ppermute | solution.py:23
  221.4 7.3 %collective-permute-start.8 = (f32[16,512]{1,0:T(8,128)S(1)}, f32[16,512]{1,0:T(8,128)S(1)}, u32[]{:S(2)}, u32[]{:S(2)}) collective-permute-start(f32[16,512]{1,0:T(8,128)S(1)} %add.66), channel_id=1, source_target_pairs={{0,4},{1,5},{2,6},{3,7},{4,0},{5,1},{6,2},{7,3},{8,12},{9,13},{10,... | collective-permute-start | bytes 98312 | tf_op jit(solution)/shard_map/ppermute | solution.py:23
  229.4 177.2 %all-gather.15.cloned.1.call-start = ((), (), s32[]{:S(2)}) async-start(), calls=%async_computation.4 | async-start | bytes 1064960 | tf_op jit(solution)/shard_map/all_gather | solution.py:27
  310.5 3.1 collective-permute-start.9
  313.6 5.8 %collective-permute-start.10 = (f32[16,512]{1,0:T(8,128)S(1)}, f32[16,512]{1,0:T(8,128)S(1)}, u32[]{:S(2)}, u32[]{:S(2)}) collective-permute-start(f32[16,512]{1,0:T(8,128)S(1)} %add.71), channel_id=1, source_target_pairs={{0,2},{1,3},{2,0},{3,1},{4,6},{5,7},{6,4},{7,5},{8,10},{9,11},{10,... | collective-permute-start | bytes 98312 | tf_op jit(solution)/shard_map/ppermute | solution.py:23
  319.4 7.3 %collective-permute-start.11 = (f32[16,512]{1,0:T(8,128)S(1)}, f32[16,512]{1,0:T(8,128)S(1)}, u32[]{:S(2)}, u32[]{:S(2)}) collective-permute-start(f32[16,512]{1,0:T(8,128)S(1)} %add.72), channel_id=1, source_target_pairs={{0,4},{1,5},{2,6},{3,7},{4,0},{5,1},{6,2},{7,3},{8,12},{9,13},{10,... | collective-permute-start | bytes 98312 | tf_op jit(solution)/shard_map/ppermute | solution.py:23
  327.3 125.3 %reduce-scatter.2.cloned.1.call-start = ((), (), s32[]{:S(2)}) async-start(), calls=%async_computation.5 | async-start | bytes 4718592 | tf_op jit(solution)/shard_map/reduce_scatter | solution.py:36
Sparse Core Ops, SparseCore 0:
  26.6 86.0 all-gather.8
  131.5 79.0 all-gather.10
  229.5 79.0 all-gather.12
  327.4 79.0 all-gather.14
  411.7 40.8 reduce-scatter.1
